TPU v7x, 32 devices: a whole 2x2x4 slice. The times are simulated.
32 devices in a mesh: grp: 2 (over y), inp: 4 (over z), tm: 2 (over x), pol: 2 (over core).
Axes of the slice: x: 2, y: 2, z: 4, core: 2. Of those that a mesh axis runs over, the one named last changes fastest.
Arguments:
- samples: bfloat16 [512, 64, 4096], P(('grp', 'inp'), ('tm', 'pol')), parts along dimension 0, may hold values from -6 to 6
- coefficients: float32 [16, 4096], replicated, may hold values from -1.5 to 1.5
Outputs:
- visibilities: float32 [4096, 256, 256], P(('grp', 'inp', 'tm', 'pol')), parts along dimension 0
There are 2 independent parts, one for each index of `grp`. A program takes and returns all parts, laid end to end along the dimension named above; an argument that names none is the same for every part. Nothing has to cross between parts.
All inputs are finite; a program needn't handle non-finite values.
Results may differ from a plain program's by a relative error of at most 0.0034.
Values may be sent and summed in bfloat16 or wider, within the bound.
No kernel may reach another device: no remote copies, remote signals or barrier semaphores. Data moves between devices by JAX's collectives and lax.ppermute only.
A program may use at most 256 MiB of HBM per device.

v0:
```python
import math
import jax
import jax.numpy as jnp
from jax import lax
from jax.sharding import PartitionSpec as P


def from_behind(block, axis, distance):
    devices = range(lax.axis_size(axis))
    route = [(i - distance, i) for i in devices if i - distance in devices]
    return lax.ppermute(block, axis, route)


def correlate(real_part, imag_part, total_frames):
    joined = jnp.concatenate([real_part, imag_part], axis=2)
    turned = jnp.concatenate([imag_part, -real_part], axis=2)
    stacked = jnp.concatenate([joined, turned], axis=1)
    product = jnp.einsum("cif,cjf->cij", stacked, joined, preferred_element_type=jnp.float32)
    width = real_part.shape[1]
    row_index = lax.broadcasted_iota(jnp.int32, (width, width), 0)
    col_index = lax.broadcasted_iota(jnp.int32, (width, width), 1)
    packed = jnp.where(row_index <= col_index, product[:, :width], product[:, width:])
    return packed * (1.0 / total_frames)


def filter_frames(block, coefficients, taps):
    frame_count = block.shape[1] - taps + 1
    total = jnp.zeros((block.shape[0], frame_count, block.shape[2]), jnp.float32)
    for tap_index in range(taps):
        total = total + coefficients[tap_index] * block[
            :, tap_index : tap_index + frame_count
        ].astype(jnp.float32)
    return total


def angles(first_idx, second_idx, period):
    product = first_idx[:, None] * second_idx[None, :] % period
    return product.astype(jnp.float32) * (2.0 * math.pi / period)


def transform(filtered):
    row_total, length = filtered.shape
    inner_len = 2 ** ((length.bit_length() - 1) // 2)
    outer_len = length // inner_len
    blocks = filtered.reshape(row_total, inner_len, outer_len)
    inner_idx = jnp.arange(inner_len, dtype=jnp.int32)
    outer_idx = jnp.arange(outer_len, dtype=jnp.int32)
    half_idx = jnp.arange(outer_len // 2, dtype=jnp.int32)
    angle_one = angles(inner_idx, inner_idx, inner_len)
    table_one = jnp.concatenate([jnp.cos(angle_one), -jnp.sin(angle_one)], axis=1)
    section_one = jnp.einsum("rab,ak->rbk", blocks, table_one, precision=lax.Precision.HIGHEST)
    first_re = section_one[..., :inner_len]
    first_im = section_one[..., inner_len:]
    angle_twist = angles(outer_idx, inner_idx, length)
    twist_cos = jnp.cos(angle_twist)
    twist_sin = jnp.sin(angle_twist)
    turned_re = first_re * twist_cos + first_im * twist_sin
    turned_im = first_im * twist_cos - first_re * twist_sin
    angle_two = angles(outer_idx, half_idx, outer_len)
    table_cos = jnp.cos(angle_two)
    table_sin = jnp.sin(angle_two)
    highest = lax.Precision.HIGHEST
    out_re = jnp.einsum("rbk,bq->qkr", turned_re, table_cos, precision=highest) + jnp.einsum(
        "rbk,bq->qkr", turned_im, table_sin, precision=highest
    )
    out_im = jnp.einsum("rbk,bq->qkr", turned_im, table_cos, precision=highest) - jnp.einsum(
        "rbk,bq->qkr", turned_re, table_sin, precision=highest
    )
    scale_factor = 1.0 / math.sqrt(length)
    return jnp.stack([out_re, out_im]).reshape(2, length // 2, row_total) * scale_factor


def per_device(samples, coefficients):
    in_dev, frame_count, length = samples.shape
    taps = coefficients.shape[0]
    channels = length // 2
    history = from_behind(samples[:, frame_count - taps + 1 :, :], ("tm", "pol"), 1)
    extended = jnp.concatenate([history, samples], axis=1)
    group_size = math.gcd(in_dev, 4)
    spectra_buf = jnp.zeros((2, channels, in_dev, frame_count), jnp.bfloat16)

    def one_group(group_index, buffer_now):
        block = lax.dynamic_slice_in_dim(extended, group_index * group_size, group_size, 0)
        filtered = filter_frames(block, coefficients, taps).reshape(
            group_size * frame_count, length
        )
        spectra_grp = (
            transform(filtered).reshape(2, channels, group_size, frame_count).astype(jnp.bfloat16)
        )
        return lax.dynamic_update_slice_in_dim(buffer_now, spectra_grp, group_index * group_size, 2)

    local_spec = lax.fori_loop(0, in_dev // group_size, one_group, spectra_buf)
    n_inputs = lax.axis_size("inp")
    n_blocks = lax.axis_size("tm")
    n_halves = lax.axis_size("pol")
    total_frames = frame_count * n_blocks * n_halves
    arrived = lax.all_to_all(
        local_spec[None], ("inp", "tm", "pol"), split_axis=2, concat_axis=0, tiled=True
    )
    width = arrived.shape[2]
    arrived = arrived.reshape(n_inputs, n_blocks * n_halves, 2, width, in_dev, frame_count)
    arrived = jnp.transpose(arrived, (2, 3, 0, 4, 1, 5)).reshape(
        2, width, n_inputs * in_dev, n_blocks * n_halves * frame_count
    )
    return correlate(arrived[0], arrived[1], total_frames)


def solution(mesh):
    placed = (P(("grp", "inp"), ("tm", "pol"), None), P())
    return jax.shard_map(
        per_device,
        mesh=mesh,
        in_specs=placed,
        out_specs=P(("grp", "inp", "tm", "pol"), None, None),
        check_vma=False,
    )
```

profile of v0, /device:TPU:11, one launch (start us, length us, event | category | flops | bytes accessed | tf_op | source)
XLA Modules:
  0.0 989.7 jit_solution(8066666141013795568)
XLA Ops:
  0.0 10.5 %slice.391 = bf16[64,15,4096]{2,1,0:T(8,128)(2,1)} slice(bf16[64,16,4096]{2,1,0:T(8,128)(2,1)} %param.4), slice={[0:64], [1:16], [0:4096]} | slice | bytes 15728640 | tf_op jit(solution)/shard_map/slice | solution.py:77
  10.5 11.0 %copy.61 = bf16[64,15,4096]{2,0,1:T(8,128)(2,1)} copy(bf16[64,15,4096]{2,1,0:T(8,128)(2,1)} %slice.391) | data formatting | bytes 15728640
  23.3 13.1 %collective-permute-done = bf16[64,15,4096]{2,0,1:T(8,128)(2,1)} collective-permute-done((bf16[64,15,4096]{2,0,1:T(8,128)(2,1)}, bf16[64,15,4096]{2,0,1:T(8,128)(2,1)}, u32[]{:S(2)}, u32[]{:S(2)}) %collective-permute-start) | collective-permute-done | bytes 7864352 | tf_op jit(solution)/shard_map/ppermute | solution.py:11
  36.3 10.8 %copy.45 = bf16[64,15,4096]{2,1,0:T(8,128)(2,1)} copy(bf16[64,15,4096]{2,0,1:T(8,128)(2,1)} %collective-permute-done) | data formatting | bytes 15728640 | tf_op jit(solution)/shard_map/ppermute | solution.py:11
  47.1 14.9 %pad_maximum_fusion = bf16[64,31,4096]{2,1,0:T(8,128)(2,1)} fusion(bf16[64,16,4096]{2,1,0:T(8,128)(2,1)} %param.4, bf16[64,15,4096]{2,1,0:T(8,128)(2,1)} %copy.45), kind=kLoop, calls=%fused_computation.71 | loop fusion | flops 32505856 | bytes 32505856 | tf_op jit(solution)/shard_map/concatenate | solution.py:78
  66.4 447.3 %while.16 = (s32[]{:T(128)}, bf16[2,2048,64,16]{1,3,2,0:T(8,128)(2,1)}, f32[16,4096]{1,0:T(8,128)S(1)}, bf16[64,31,4096]{2,1,0:T(8,128)(2,1)}, s32[]{:T(128)}, /...) while((s32[]{:T(128)}, ...), condition=%wide.region_1.2_spmd, body=%wide.region_0.1_spmd.sunk | while | flops 822063104 | bytes 40468980 | solution.py:92
  67.1 10.2 %multiply_add_fusion.9 = f32[4,16,4096]{2,1,0:T(8,128)S(1)} fusion(bf16[64,31,4096]{2,1,0:T(8,128)(2,1)} %get-tuple-element.280, s32[]{:T(128)S(6)} %select_n.151, s32[]{:T(128)S(6)} %add.431, s32[]{:T(128)S(6)} %add.432, s32[]{:T(128)S(6)} %add.433, s32[]{:T(128)S(6)} %add.434, s32[]{:T(128)S(6)} %add.435, s32[]{:T(128)S(6)} %add.436, s32[]{:T(128)S(6)} %add.437, ...), kind=kLoop, calls=%fused_computation.8.clone.1 | loop fusion | flops 12320768 | bytes 9699392 | tf_op jit(solution)/shard_map/while/body/eval_jaxpr/add | solution.py:30
  95.0 9.7 multiply_add_fusion.9
  122.4 10.7 %multiply_add_fusion.9 = f32[4,16,4096]{2,1,0:T(8,128)S(1)} fusion(bf16[64,31,4096]{2,1,0:T(8,128)(2,1)} %get-tuple-element.280, s32[]{:T(128)S(6)} %select_n.151, s32[]{:T(128)S(6)} %add.431, s32[]{:T(128)S(6)} %add.432, s32[]{:T(128)S(6)} %add.433, s32[]{:T(128)S(6)} %add.434, s32[]{:T(128)S(6)} %add.435, s32[]{:T(128)S(6)} %add.436, s32[]{:T(128)S(6)} %add.437, ...), kind=kLoop, calls=%fused_computation.8.clone.1 | loop fusion | flops 12320768 | bytes 9699392 | tf_op jit(solution)/shard_map/while/body/eval_jaxpr/add | solution.py:30
  150.9 9.9 %multiply_add_fusion.9 = f32[4,16,4096]{2,1,0:T(8,128)S(1)} fusion(bf16[64,31,4096]{2,1,0:T(8,128)(2,1)} %get-tuple-element.280, s32[]{:T(128)S(6)} %select_n.151, s32[]{:T(128)S(6)} %add.431, s32[]{:T(128)S(6)} %add.432, s32[]{:T(128)S(6)} %add.433, s32[]{:T(128)S(6)} %add.434, s32[]{:T(128)S(6)} %add.435, s32[]{:T(128)S(6)} %add.436, s32[]{:T(128)S(6)} %add.437, ...), kind=kLoop, calls=%fused_computation.8.clone.1 | loop fusion | flops 12320768 | bytes 9699392 | tf_op jit(solution)/shard_map/while/body/eval_jaxpr/add | solution.py:30
  178.5 9.5 multiply_add_fusion.9
  205.8 10.1 %multiply_add_fusion.9 = f32[4,16,4096]{2,1,0:T(8,128)S(1)} fusion(bf16[64,31,4096]{2,1,0:T(8,128)(2,1)} %get-tuple-element.280, s32[]{:T(128)S(6)} %select_n.151, s32[]{:T(128)S(6)} %add.431, s32[]{:T(128)S(6)} %add.432, s32[]{:T(128)S(6)} %add.433, s32[]{:T(128)S(6)} %add.434, s32[]{:T(128)S(6)} %add.435, s32[]{:T(128)S(6)} %add.436, s32[]{:T(128)S(6)} %add.437, ...), kind=kLoop, calls=%fused_computation.8.clone.1 | loop fusion | flops 12320768 | bytes 9699392 | tf_op jit(solution)/shard_map/while/body/eval_jaxpr/add | solution.py:30
  233.6 10.9 %multiply_add_fusion.9 = f32[4,16,4096]{2,1,0:T(8,128)S(1)} fusion(bf16[64,31,4096]{2,1,0:T(8,128)(2,1)} %get-tuple-element.280, s32[]{:T(128)S(6)} %select_n.151, s32[]{:T(128)S(6)} %add.431, s32[]{:T(128)S(6)} %add.432, s32[]{:T(128)S(6)} %add.433, s32[]{:T(128)S(6)} %add.434, s32[]{:T(128)S(6)} %add.435, s32[]{:T(128)S(6)} %add.436, s32[]{:T(128)S(6)} %add.437, ...), kind=kLoop, calls=%fused_computation.8.clone.1 | loop fusion | flops 12320768 | bytes 9699392 | tf_op jit(solution)/shard_map/while/body/eval_jaxpr/add | solution.py:30
  262.3 9.6 multiply_add_fusion.9
  289.6 10.2 %multiply_add_fusion.9 = f32[4,16,4096]{2,1,0:T(8,128)S(1)} fusion(bf16[64,31,4096]{2,1,0:T(8,128)(2,1)} %get-tuple-element.280, s32[]{:T(128)S(6)} %select_n.151, s32[]{:T(128)S(6)} %add.431, s32[]{:T(128)S(6)} %add.432, s32[]{:T(128)S(6)} %add.433, s32[]{:T(128)S(6)} %add.434, s32[]{:T(128)S(6)} %add.435, s32[]{:T(128)S(6)} %add.436, s32[]{:T(128)S(6)} %add.437, ...), kind=kLoop, calls=%fused_computation.8.clone.1 | loop fusion | flops 12320768 | bytes 9699392 | tf_op jit(solution)/shard_map/while/body/eval_jaxpr/add | solution.py:30
  317.5 9.8 multiply_add_fusion.9
  345.0 10.2 %multiply_add_fusion.9 = f32[4,16,4096]{2,1,0:T(8,128)S(1)} fusion(bf16[64,31,4096]{2,1,0:T(8,128)(2,1)} %get-tuple-element.280, s32[]{:T(128)S(6)} %select_n.151, s32[]{:T(128)S(6)} %add.431, s32[]{:T(128)S(6)} %add.432, s32[]{:T(128)S(6)} %add.433, s32[]{:T(128)S(6)} %add.434, s32[]{:T(128)S(6)} %add.435, s32[]{:T(128)S(6)} %add.436, s32[]{:T(128)S(6)} %add.437, ...), kind=kLoop, calls=%fused_computation.8.clone.1 | loop fusion | flops 12320768 | bytes 9699392 | tf_op jit(solution)/shard_map/while/body/eval_jaxpr/add | solution.py:30
  373.0 10.8 %multiply_add_fusion.9 = f32[4,16,4096]{2,1,0:T(8,128)S(1)} fusion(bf16[64,31,4096]{2,1,0:T(8,128)(2,1)} %get-tuple-element.280, s32[]{:T(128)S(6)} %select_n.151, s32[]{:T(128)S(6)} %add.431, s32[]{:T(128)S(6)} %add.432, s32[]{:T(128)S(6)} %add.433, s32[]{:T(128)S(6)} %add.434, s32[]{:T(128)S(6)} %add.435, s32[]{:T(128)S(6)} %add.436, s32[]{:T(128)S(6)} %add.437, ...), kind=kLoop, calls=%fused_computation.8.clone.1 | loop fusion | flops 12320768 | bytes 9699392 | tf_op jit(solution)/shard_map/while/body/eval_jaxpr/add | solution.py:30
  401.5 10.7 %multiply_add_fusion.9 = f32[4,16,4096]{2,1,0:T(8,128)S(1)} fusion(bf16[64,31,4096]{2,1,0:T(8,128)(2,1)} %get-tuple-element.280, s32[]{:T(128)S(6)} %select_n.151, s32[]{:T(128)S(6)} %add.431, s32[]{:T(128)S(6)} %add.432, s32[]{:T(128)S(6)} %add.433, s32[]{:T(128)S(6)} %add.434, s32[]{:T(128)S(6)} %add.435, s32[]{:T(128)S(6)} %add.436, s32[]{:T(128)S(6)} %add.437, ...), kind=kLoop, calls=%fused_computation.8.clone.1 | loop fusion | flops 12320768 | bytes 9699392 | tf_op jit(solution)/shard_map/while/body/eval_jaxpr/add | solution.py:30
  430.0 10.3 %multiply_add_fusion.9 = f32[4,16,4096]{2,1,0:T(8,128)S(1)} fusion(bf16[64,31,4096]{2,1,0:T(8,128)(2,1)} %get-tuple-element.280, s32[]{:T(128)S(6)} %select_n.151, s32[]{:T(128)S(6)} %add.431, s32[]{:T(128)S(6)} %add.432, s32[]{:T(128)S(6)} %add.433, s32[]{:T(128)S(6)} %add.434, s32[]{:T(128)S(6)} %add.435, s32[]{:T(128)S(6)} %add.436, s32[]{:T(128)S(6)} %add.437, ...), kind=kLoop, calls=%fused_computation.8.clone.1 | loop fusion | flops 12320768 | bytes 9699392 | tf_op jit(solution)/shard_map/while/body/eval_jaxpr/add | solution.py:30
  458.0 10.4 %multiply_add_fusion.9 = f32[4,16,4096]{2,1,0:T(8,128)S(1)} fusion(bf16[64,31,4096]{2,1,0:T(8,128)(2,1)} %get-tuple-element.280, s32[]{:T(128)S(6)} %select_n.151, s32[]{:T(128)S(6)} %add.431, s32[]{:T(128)S(6)} %add.432, s32[]{:T(128)S(6)} %add.433, s32[]{:T(128)S(6)} %add.434, s32[]{:T(128)S(6)} %add.435, s32[]{:T(128)S(6)} %add.436, s32[]{:T(128)S(6)} %add.437, ...), kind=kLoop, calls=%fused_computation.8.clone.1 | loop fusion | flops 12320768 | bytes 9699392 | tf_op jit(solution)/shard_map/while/body/eval_jaxpr/add | solution.py:30
  486.1 10.1 %multiply_add_fusion.9 = f32[4,16,4096]{2,1,0:T(8,128)S(1)} fusion(bf16[64,31,4096]{2,1,0:T(8,128)(2,1)} %get-tuple-element.280, s32[]{:T(128)S(6)} %select_n.151, s32[]{:T(128)S(6)} %add.431, s32[]{:T(128)S(6)} %add.432, s32[]{:T(128)S(6)} %add.433, s32[]{:T(128)S(6)} %add.434, s32[]{:T(128)S(6)} %add.435, s32[]{:T(128)S(6)} %add.436, s32[]{:T(128)S(6)} %add.437, ...), kind=kLoop, calls=%fused_computation.8.clone.1 | loop fusion | flops 12320768 | bytes 9699392 | tf_op jit(solution)/shard_map/while/body/eval_jaxpr/add | solution.py:30
  513.6 28.6 %copy.46 = bf16[2,2048,64,16]{2,3,0,1:T(8,128)(2,1)} copy(bf16[2,2048,64,16]{1,3,2,0:T(8,128)(2,1)} %get-tuple-element.135) | data formatting | bytes 16777216 | tf_op jit(solution)/shard_map/while | solution.py:92
  542.2 14.5 %bitcast_bitcast_fusion = bf16[2048,1,2,16,64]{4,3,2,1,0:T(8,128)(2,1)} fusion(bf16[2,2048,64,16]{2,3,0,1:T(8,128)(2,1)} %copy.46), kind=kLoop, calls=%fused_computation.87 | loop fusion | bytes 16777216
  556.7 19.6 %reshape.97 = bf16[16,2,131072]{2,1,0:T(2,128)(2,1)} reshape(bf16[2048,1,2,16,64]{4,3,2,1,0:T(8,128)(2,1)} %bitcast_bitcast_fusion) | data formatting | bytes 16777216
  576.4 81.2 %all-to-all-start = ((bf16[16,2,131072]{2,1,0:T(2,128)(2,1)}), bf16[16,2,131072]{2,1,0:T(2,128)(2,1)}, u32[]{:S(2)}, u32[]{:S(2)}) async-start(bf16[16,2,131072]{2,1,0:T(2,128)(2,1)} %reshape.97), calls=%async_computation | async-start | bytes 16777216 | tf_op jit(solution)/shard_map/all_to_all | solution.py:97
  657.6 182.3 %all-to-all-done = bf16[16,2,131072]{2,1,0:T(2,128)(2,1)} async-done(((bf16[16,2,131072]{2,1,0:T(2,128)(2,1)}), bf16[16,2,131072]{2,1,0:T(2,128)(2,1)}, u32[]{:S(2)}, u32[]{:S(2)}) %all-to-all-start) | async-done | bytes 8388640 | tf_op jit(solution)/shard_map/all_to_all | solution.py:97
  839.9 19.2 %reshape.98 = bf16[2048,1,2,16,64]{4,3,2,1,0:T(8,128)(2,1)} reshape(bf16[16,2,131072]{2,1,0:T(2,128)(2,1)} %all-to-all-done) | data formatting | bytes 16777216
  859.1 20.7 %copy.60 = bf16[1,2,16,128,64,16]{3,2,5,4,1,0:T(8,128)(2,1)} copy(bf16[1,2,16,128,64,16]{4,5,1,3,2,0:T(8,128)(2,1)} %bitcast.98) | data formatting | bytes 16777216 | tf_op jit(solution)/shard_map/all_to_all | solution.py:97
  879.8 8.9 copy.48
  923.2 32.7 %fusion.57 = f32[128,512,256]{2,1,0:T(8,128)} fusion(bf16[128,256,64]{1,2,0:T(8,128)(2,1)} %neg.14, bf16[128,256,64]{1,2,0:T(8,128)(2,1)} %copy.52, bf16[128,256,64]{1,2,0:T(8,128)(2,1)} %copy.51), kind=kOutput, calls=%fused_computation.72 | convolution fusion | flops 4378853376 | bytes 79691776 | tf_op jit(solution)/shard_map/cif,cjf->cij/dot_general | solution.py:18
  955.9 33.5 %fusion.56 = f32[128,256,256]{2,1,0:T(8,128)} fusion(f32[128,512,256]{2,1,0:T(8,128)} %fusion.57, pred[256,256]{1,0:T(8,128)(4,1)S(1)} %iota_compare_fusion), kind=kLoop, calls=%fused_computation.70 | loop fusion | flops 16777216 | bytes 100728832 | tf_op jit(solution)/shard_map/mul | solution.py:23
  (203 shorter events, 323.1 us)
Async XLA Ops:
  21.5 14.8 %collective-permute-start = (bf16[64,15,4096]{2,0,1:T(8,128)(2,1)}, bf16[64,15,4096]{2,0,1:T(8,128)(2,1)}, u32[]{:S(2)}, u32[]{:S(2)}) collective-permute-start(bf16[64,15,4096]{2,0,1:T(8,128)(2,1)} %copy.61), channel_id=1, source_target_pairs={{0,1},{1,2},{2,3},{4,5},{5,6},{6,7},{8,9},{9,10},{10,11},{12,13},{... | collective-permute-start | bytes 23592968 | tf_op jit(solution)/shard_map/ppermute | solution.py:11
  62.1 4.3 copy-start
  576.4 263.5 %all-to-all-start = ((bf16[16,2,131072]{2,1,0:T(2,128)(2,1)}), bf16[16,2,131072]{2,1,0:T(2,128)(2,1)}, u32[]{:S(2)}, u32[]{:S(2)}) async-start(bf16[16,2,131072]{2,1,0:T(2,128)(2,1)} %reshape.97), calls=%async_computation | async-start | bytes 16777216 | tf_op jit(solution)/shard_map/all_to_all | solution.py:97
where the time goes:
time: 999 us; the launch traced here: 990 us
  other arithmetic  252 us (25%)
  local copies, waits for them, and re-layouts  241 us (24%)
  matrix products  216 us (22%)
  waiting for transfers between devices  195 us (20%)
  starting transfers between devices  82.9 us (8%)
    all_to_all x1, waiting for transfers between devices, per_device(): lax.all_to_all(local_spec[None], ('inp', 'tm', 'pol'), split_axis=2, conc...  182 us
    add x16, other arithmetic, filter_frames(): total + coefficients[tap_index] * block[:, tap_index:tap_index + frame_co...  163 us
    all_to_all x1, starting transfers between devices, per_device(): lax.all_to_all(local_spec[None], ('inp', 'tm', 'pol'), split_axis=2, conc...  81.2 us
    dot_general x16, matrix products, transform(): jnp.einsum('rab,ak->rbk', blocks, table_one, precision=lax.Precision.HIGH...  80.8 us
    unnamed x6, local copies, waits for them, and re-layouts  64.4 us
    reshape x16, local copies, waits for them, and re-layouts, transform(): blocks = filtered.reshape(row_total, inner_len, outer_len)  35.3 us
    mul x1, other arithmetic, correlate(): return packed * (1.0 / total_frames)  33.5 us
    dot_general x1, matrix products, correlate(): jnp.einsum('cif,cjf->cij', stacked, joined, preferred_element_type=jnp.fl...  32.7 us
  transfers between devices with their start and end apart: 2, of which 2 were waited for; matrix products, arithmetic and copies ran while one was open for 0% of the time, Pallas kernels for 0%

commit v1 on v0

--- a/solution.py
+++ b/solution.py
@@ -94,8 +94,14 @@
     n_blocks = lax.axis_size("tm")
     n_halves = lax.axis_size("pol")
     total_frames = frame_count * n_blocks * n_halves
-    arrived = lax.all_to_all(
-        local_spec[None], ("inp", "tm", "pol"), split_axis=2, concat_axis=0, tiled=True
+    arrived = jnp.concatenate(
+        lax.all_to_all(
+            jnp.stack(jnp.split(local_spec[None], lax.axis_size(("inp", "tm", "pol")), axis=2)),
+            ("inp", "tm", "pol"),
+            0,
+            0,
+        ),
+        axis=0,
     )
     width = arrived.shape[2]
     arrived = arrived.reshape(n_inputs, n_blocks * n_halves, 2, width, in_dev, frame_count)

time: 999 us -> 910 us (0.911)
  local copies, waits for them, and re-layouts: 241 us -> 152 us
    unnamed x6 -> x20, local copies, waits for them, and re-layouts: 64.4 us -> 33.4 us
    all_to_all x2 -> x0, local copies, waits for them, and re-layouts: 29.7 us -> none  [per_device(): lax.all_to_all(local_spec[None], ('inp', 'tm', 'pol'), split_axis=2, conc...]
    while x1 -> x0, local copies, waits for them, and re-layouts: 28.6 us -> none  [per_device(): local_spec = lax.fori_loop(0, in_dev // group_size, one_group, spectra_buf)]
where the time goes in v1:
time: 910 us; the launch traced here: 901 us
  other arithmetic  252 us (28%)
  matrix products  217 us (24%)
  waiting for transfers between devices  195 us (21%)
  local copies, waits for them, and re-layouts  152 us (17%)
  starting transfers between devices  82.9 us (9%)
    all_to_all x1, waiting for transfers between devices, per_device(): lax.all_to_all(jnp.stack(jnp.split(local_spec[None], lax.axis_size(('inp'...  182 us
    add x16, other arithmetic, filter_frames(): total + coefficients[tap_index] * block[:, tap_index:tap_index + frame_co...  163 us
    all_to_all x1, starting transfers between devices, per_device(): lax.all_to_all(jnp.stack(jnp.split(local_spec[None], lax.axis_size(('inp'...  81.2 us
    dot_general x16, matrix products, transform(): jnp.einsum('rab,ak->rbk', blocks, table_one, precision=lax.Precision.HIGH...  80.8 us
    reshape x16, local copies, waits for them, and re-layouts, transform(): blocks = filtered.reshape(row_total, inner_len, outer_len)  35.2 us
    mul x1, other arithmetic, correlate(): return packed * (1.0 / total_frames)  33.5 us
    unnamed x20, local copies, waits for them, and re-layouts  33.4 us
    dot_general x1, matrix products, correlate(): jnp.einsum('cif,cjf->cij', stacked, joined, preferred_element_type=jnp.fl...  32.8 us
  transfers between devices with their start and end apart: 2, of which 2 were waited for; matrix products, arithmetic and copies ran while one was open for 0% of the time, Pallas kernels for 0%

profile of v1, /device:TPU:11, one launch (start us, length us, event | category | flops | bytes accessed | tf_op | source)
XLA Modules:
  0.0 901.2 jit_solution(10642276049798151621)
XLA Ops:
  0.0 10.5 %slice.391 = bf16[64,15,4096]{2,1,0:T(8,128)(2,1)} slice(bf16[64,16,4096]{2,1,0:T(8,128)(2,1)} %param.4), slice={[0:64], [1:16], [0:4096]} | slice | bytes 15728640 | tf_op jit(solution)/shard_map/slice | solution.py:77
  10.5 11.0 %copy.40 = bf16[64,15,4096]{2,0,1:T(8,128)(2,1)} copy(bf16[64,15,4096]{2,1,0:T(8,128)(2,1)} %slice.391) | data formatting | bytes 15728640
  23.3 13.1 %collective-permute-done = bf16[64,15,4096]{2,0,1:T(8,128)(2,1)} collective-permute-done((bf16[64,15,4096]{2,0,1:T(8,128)(2,1)}, bf16[64,15,4096]{2,0,1:T(8,128)(2,1)}, u32[]{:S(2)}, u32[]{:S(2)}) %collective-permute-start) | collective-permute-done | bytes 7864352 | tf_op jit(solution)/shard_map/ppermute | solution.py:11
  36.3 10.8 %copy.28 = bf16[64,15,4096]{2,1,0:T(8,128)(2,1)} copy(bf16[64,15,4096]{2,0,1:T(8,128)(2,1)} %collective-permute-done) | data formatting | bytes 15728640 | tf_op jit(solution)/shard_map/ppermute | solution.py:11
  47.1 14.9 %pad_maximum_fusion = bf16[64,31,4096]{2,1,0:T(8,128)(2,1)} fusion(bf16[64,16,4096]{2,1,0:T(8,128)(2,1)} %param.4, bf16[64,15,4096]{2,1,0:T(8,128)(2,1)} %copy.28), kind=kLoop, calls=%fused_computation.71 | loop fusion | flops 32505856 | bytes 32505856 | tf_op jit(solution)/shard_map/concatenate | solution.py:78
  66.3 447.3 %while.16 = (s32[]{:T(128)}, bf16[2,2048,64,16]{1,3,2,0:T(8,128)(2,1)}, f32[16,4096]{1,0:T(8,128)S(1)}, bf16[64,31,4096]{2,1,0:T(8,128)(2,1)}, s32[]{:T(128)}, /...) while((s32[]{:T(128)}, ...), condition=%wide.region_1.2_spmd, body=%wide.region_0.1_spmd.sunk | while | flops 822063104 | bytes 40468980 | solution.py:92
  67.1 10.2 %multiply_add_fusion.9 = f32[4,16,4096]{2,1,0:T(8,128)S(1)} fusion(bf16[64,31,4096]{2,1,0:T(8,128)(2,1)} %get-tuple-element.280, s32[]{:T(128)S(6)} %select_n.151, s32[]{:T(128)S(6)} %add.431, s32[]{:T(128)S(6)} %add.432, s32[]{:T(128)S(6)} %add.433, s32[]{:T(128)S(6)} %add.434, s32[]{:T(128)S(6)} %add.435, s32[]{:T(128)S(6)} %add.436, s32[]{:T(128)S(6)} %add.437, ...), kind=kLoop, calls=%fused_computation.8.clone.1 | loop fusion | flops 12320768 | bytes 9699392 | tf_op jit(solution)/shard_map/while/body/eval_jaxpr/add | solution.py:30
  79.5 5.0 fusion.113
  95.0 9.7 %multiply_add_fusion.9 = f32[4,16,4096]{2,1,0:T(8,128)S(1)} fusion(bf16[64,31,4096]{2,1,0:T(8,128)(2,1)} %get-tuple-element.280, s32[]{:T(128)S(6)} %select_n.151, s32[]{:T(128)S(6)} %add.431, s32[]{:T(128)S(6)} %add.432, s32[]{:T(128)S(6)} %add.433, s32[]{:T(128)S(6)} %add.434, s32[]{:T(128)S(6)} %add.435, s32[]{:T(128)S(6)} %add.436, s32[]{:T(128)S(6)} %add.437, ...), kind=kLoop, calls=%fused_computation.8.clone.1 | loop fusion | flops 12320768 | bytes 9699392 | tf_op jit(solution)/shard_map/while/body/eval_jaxpr/add | solution.py:30
  122.4 10.7 %multiply_add_fusion.9 = f32[4,16,4096]{2,1,0:T(8,128)S(1)} fusion(bf16[64,31,4096]{2,1,0:T(8,128)(2,1)} %get-tuple-element.280, s32[]{:T(128)S(6)} %select_n.151, s32[]{:T(128)S(6)} %add.431, s32[]{:T(128)S(6)} %add.432, s32[]{:T(128)S(6)} %add.433, s32[]{:T(128)S(6)} %add.434, s32[]{:T(128)S(6)} %add.435, s32[]{:T(128)S(6)} %add.436, s32[]{:T(128)S(6)} %add.437, ...), kind=kLoop, calls=%fused_computation.8.clone.1 | loop fusion | flops 12320768 | bytes 9699392 | tf_op jit(solution)/shard_map/while/body/eval_jaxpr/add | solution.py:30
  150.8 9.9 %multiply_add_fusion.9 = f32[4,16,4096]{2,1,0:T(8,128)S(1)} fusion(bf16[64,31,4096]{2,1,0:T(8,128)(2,1)} %get-tuple-element.280, s32[]{:T(128)S(6)} %select_n.151, s32[]{:T(128)S(6)} %add.431, s32[]{:T(128)S(6)} %add.432, s32[]{:T(128)S(6)} %add.433, s32[]{:T(128)S(6)} %add.434, s32[]{:T(128)S(6)} %add.435, s32[]{:T(128)S(6)} %add.436, s32[]{:T(128)S(6)} %add.437, ...), kind=kLoop, calls=%fused_computation.8.clone.1 | loop fusion | flops 12320768 | bytes 9699392 | tf_op jit(solution)/shard_map/while/body/eval_jaxpr/add | solution.py:30
  178.5 9.5 %multiply_add_fusion.9 = f32[4,16,4096]{2,1,0:T(8,128)S(1)} fusion(bf16[64,31,4096]{2,1,0:T(8,128)(2,1)} %get-tuple-element.280, s32[]{:T(128)S(6)} %select_n.151, s32[]{:T(128)S(6)} %add.431, s32[]{:T(128)S(6)} %add.432, s32[]{:T(128)S(6)} %add.433, s32[]{:T(128)S(6)} %add.434, s32[]{:T(128)S(6)} %add.435, s32[]{:T(128)S(6)} %add.436, s32[]{:T(128)S(6)} %add.437, ...), kind=kLoop, calls=%fused_computation.8.clone.1 | loop fusion | flops 12320768 | bytes 9699392 | tf_op jit(solution)/shard_map/while/body/eval_jaxpr/add | solution.py:30
  205.7 10.1 %multiply_add_fusion.9 = f32[4,16,4096]{2,1,0:T(8,128)S(1)} fusion(bf16[64,31,4096]{2,1,0:T(8,128)(2,1)} %get-tuple-element.280, s32[]{:T(128)S(6)} %select_n.151, s32[]{:T(128)S(6)} %add.431, s32[]{:T(128)S(6)} %add.432, s32[]{:T(128)S(6)} %add.433, s32[]{:T(128)S(6)} %add.434, s32[]{:T(128)S(6)} %add.435, s32[]{:T(128)S(6)} %add.436, s32[]{:T(128)S(6)} %add.437, ...), kind=kLoop, calls=%fused_computation.8.clone.1 | loop fusion | flops 12320768 | bytes 9699392 | tf_op jit(solution)/shard_map/while/body/eval_jaxpr/add | solution.py:30
  233.6 10.9 %multiply_add_fusion.9 = f32[4,16,4096]{2,1,0:T(8,128)S(1)} fusion(bf16[64,31,4096]{2,1,0:T(8,128)(2,1)} %get-tuple-element.280, s32[]{:T(128)S(6)} %select_n.151, s32[]{:T(128)S(6)} %add.431, s32[]{:T(128)S(6)} %add.432, s32[]{:T(128)S(6)} %add.433, s32[]{:T(128)S(6)} %add.434, s32[]{:T(128)S(6)} %add.435, s32[]{:T(128)S(6)} %add.436, s32[]{:T(128)S(6)} %add.437, ...), kind=kLoop, calls=%fused_computation.8.clone.1 | loop fusion | flops 12320768 | bytes 9699392 | tf_op jit(solution)/shard_map/while/body/eval_jaxpr/add | solution.py:30
  262.2 9.6 %multiply_add_fusion.9 = f32[4,16,4096]{2,1,0:T(8,128)S(1)} fusion(bf16[64,31,4096]{2,1,0:T(8,128)(2,1)} %get-tuple-element.280, s32[]{:T(128)S(6)} %select_n.151, s32[]{:T(128)S(6)} %add.431, s32[]{:T(128)S(6)} %add.432, s32[]{:T(128)S(6)} %add.433, s32[]{:T(128)S(6)} %add.434, s32[]{:T(128)S(6)} %add.435, s32[]{:T(128)S(6)} %add.436, s32[]{:T(128)S(6)} %add.437, ...), kind=kLoop, calls=%fused_computation.8.clone.1 | loop fusion | flops 12320768 | bytes 9699392 | tf_op jit(solution)/shard_map/while/body/eval_jaxpr/add | solution.py:30
  289.5 10.2 %multiply_add_fusion.9 = f32[4,16,4096]{2,1,0:T(8,128)S(1)} fusion(bf16[64,31,4096]{2,1,0:T(8,128)(2,1)} %get-tuple-element.280, s32[]{:T(128)S(6)} %select_n.151, s32[]{:T(128)S(6)} %add.431, s32[]{:T(128)S(6)} %add.432, s32[]{:T(128)S(6)} %add.433, s32[]{:T(128)S(6)} %add.434, s32[]{:T(128)S(6)} %add.435, s32[]{:T(128)S(6)} %add.436, s32[]{:T(128)S(6)} %add.437, ...), kind=kLoop, calls=%fused_computation.8.clone.1 | loop fusion | flops 12320768 | bytes 9699392 | tf_op jit(solution)/shard_map/while/body/eval_jaxpr/add | solution.py:30
  317.4 9.8 %multiply_add_fusion.9 = f32[4,16,4096]{2,1,0:T(8,128)S(1)} fusion(bf16[64,31,4096]{2,1,0:T(8,128)(2,1)} %get-tuple-element.280, s32[]{:T(128)S(6)} %select_n.151, s32[]{:T(128)S(6)} %add.431, s32[]{:T(128)S(6)} %add.432, s32[]{:T(128)S(6)} %add.433, s32[]{:T(128)S(6)} %add.434, s32[]{:T(128)S(6)} %add.435, s32[]{:T(128)S(6)} %add.436, s32[]{:T(128)S(6)} %add.437, ...), kind=kLoop, calls=%fused_computation.8.clone.1 | loop fusion | flops 12320768 | bytes 9699392 | tf_op jit(solution)/shard_map/while/body/eval_jaxpr/add | solution.py:30
  345.0 10.2 %multiply_add_fusion.9 = f32[4,16,4096]{2,1,0:T(8,128)S(1)} fusion(bf16[64,31,4096]{2,1,0:T(8,128)(2,1)} %get-tuple-element.280, s32[]{:T(128)S(6)} %select_n.151, s32[]{:T(128)S(6)} %add.431, s32[]{:T(128)S(6)} %add.432, s32[]{:T(128)S(6)} %add.433, s32[]{:T(128)S(6)} %add.434, s32[]{:T(128)S(6)} %add.435, s32[]{:T(128)S(6)} %add.436, s32[]{:T(128)S(6)} %add.437, ...), kind=kLoop, calls=%fused_computation.8.clone.1 | loop fusion | flops 12320768 | bytes 9699392 | tf_op jit(solution)/shard_map/while/body/eval_jaxpr/add | solution.py:30
  372.9 10.8 %multiply_add_fusion.9 = f32[4,16,4096]{2,1,0:T(8,128)S(1)} fusion(bf16[64,31,4096]{2,1,0:T(8,128)(2,1)} %get-tuple-element.280, s32[]{:T(128)S(6)} %select_n.151, s32[]{:T(128)S(6)} %add.431, s32[]{:T(128)S(6)} %add.432, s32[]{:T(128)S(6)} %add.433, s32[]{:T(128)S(6)} %add.434, s32[]{:T(128)S(6)} %add.435, s32[]{:T(128)S(6)} %add.436, s32[]{:T(128)S(6)} %add.437, ...), kind=kLoop, calls=%fused_computation.8.clone.1 | loop fusion | flops 12320768 | bytes 9699392 | tf_op jit(solution)/shard_map/while/body/eval_jaxpr/add | solution.py:30
  401.5 10.7 %multiply_add_fusion.9 = f32[4,16,4096]{2,1,0:T(8,128)S(1)} fusion(bf16[64,31,4096]{2,1,0:T(8,128)(2,1)} %get-tuple-element.280, s32[]{:T(128)S(6)} %select_n.151, s32[]{:T(128)S(6)} %add.431, s32[]{:T(128)S(6)} %add.432, s32[]{:T(128)S(6)} %add.433, s32[]{:T(128)S(6)} %add.434, s32[]{:T(128)S(6)} %add.435, s32[]{:T(128)S(6)} %add.436, s32[]{:T(128)S(6)} %add.437, ...), kind=kLoop, calls=%fused_computation.8.clone.1 | loop fusion | flops 12320768 | bytes 9699392 | tf_op jit(solution)/shard_map/while/body/eval_jaxpr/add | solution.py:30
  430.0 10.3 %multiply_add_fusion.9 = f32[4,16,4096]{2,1,0:T(8,128)S(1)} fusion(bf16[64,31,4096]{2,1,0:T(8,128)(2,1)} %get-tuple-element.280, s32[]{:T(128)S(6)} %select_n.151, s32[]{:T(128)S(6)} %add.431, s32[]{:T(128)S(6)} %add.432, s32[]{:T(128)S(6)} %add.433, s32[]{:T(128)S(6)} %add.434, s32[]{:T(128)S(6)} %add.435, s32[]{:T(128)S(6)} %add.436, s32[]{:T(128)S(6)} %add.437, ...), kind=kLoop, calls=%fused_computation.8.clone.1 | loop fusion | flops 12320768 | bytes 9699392 | tf_op jit(solution)/shard_map/while/body/eval_jaxpr/add | solution.py:30
  458.0 10.4 %multiply_add_fusion.9 = f32[4,16,4096]{2,1,0:T(8,128)S(1)} fusion(bf16[64,31,4096]{2,1,0:T(8,128)(2,1)} %get-tuple-element.280, s32[]{:T(128)S(6)} %select_n.151, s32[]{:T(128)S(6)} %add.431, s32[]{:T(128)S(6)} %add.432, s32[]{:T(128)S(6)} %add.433, s32[]{:T(128)S(6)} %add.434, s32[]{:T(128)S(6)} %add.435, s32[]{:T(128)S(6)} %add.436, s32[]{:T(128)S(6)} %add.437, ...), kind=kLoop, calls=%fused_computation.8.clone.1 | loop fusion | flops 12320768 | bytes 9699392 | tf_op jit(solution)/shard_map/while/body/eval_jaxpr/add | solution.py:30
  486.1 10.1 %multiply_add_fusion.9 = f32[4,16,4096]{2,1,0:T(8,128)S(1)} fusion(bf16[64,31,4096]{2,1,0:T(8,128)(2,1)} %get-tuple-element.280, s32[]{:T(128)S(6)} %select_n.151, s32[]{:T(128)S(6)} %add.431, s32[]{:T(128)S(6)} %add.432, s32[]{:T(128)S(6)} %add.433, s32[]{:T(128)S(6)} %add.434, s32[]{:T(128)S(6)} %add.435, s32[]{:T(128)S(6)} %add.436, s32[]{:T(128)S(6)} %add.437, ...), kind=kLoop, calls=%fused_computation.8.clone.1 | loop fusion | flops 12320768 | bytes 9699392 | tf_op jit(solution)/shard_map/while/body/eval_jaxpr/add | solution.py:30
  537.0 81.2 %all-to-all-start = ((bf16[16,1,2,128,64,16]{3,5,4,2,1,0:T(8,128)(2,1)}), bf16[16,1,2,128,64,16]{3,5,4,2,1,0:T(8,128)(2,1)}, u32[]{:S(2)}, u32[]{:S(2)}) async-start(bf16[16,1,2,128,64,16]{3,5,4,2,1,0:T(8,128)(2,1)} %fusion.68), calls=%async_computation | async-start | bytes 16777216 | tf_op jit(solution)/shard_map/all_to_all | solution.py:98
  618.2 182.3 %all-to-all-done = bf16[16,1,2,128,64,16]{3,5,4,2,1,0:T(8,128)(2,1)} async-done(((bf16[16,1,2,128,64,16]{3,5,4,2,1,0:T(8,128)(2,1)}), bf16[16,1,2,128,64,16]{3,5,4,2,1,0:T(8,128)(2,1)}, u32[]{:S(2)}, u32[]{:S(2)}) %all-to-all-start) | async-done | bytes 8388640 | tf_op jit(solution)/shard_map/all_to_all | solution.py:98
  800.5 5.5 fusion.86
  809.2 7.4 copy.32
  816.6 5.4 copy.29
  821.9 7.3 copy.31
  829.2 5.5 neg.14
  834.7 32.8 %fusion.57 = f32[128,512,256]{2,1,0:T(8,128)} fusion(bf16[128,256,64]{1,2,0:T(8,128)(2,1)} %neg.14, bf16[128,256,64]{1,2,0:T(8,128)(2,1)} %copy.32, bf16[128,256,64]{1,2,0:T(8,128)(2,1)} %copy.31), kind=kOutput, calls=%fused_computation.72 | convolution fusion | flops 4378853376 | bytes 79691776 | tf_op jit(solution)/shard_map/cif,cjf->cij/dot_general | solution.py:18
  867.5 33.5 %fusion.56 = f32[128,256,256]{2,1,0:T(8,128)} fusion(f32[128,512,256]{2,1,0:T(8,128)} %fusion.57, pred[256,256]{1,0:T(8,128)(4,1)S(1)} %iota_compare_fusion), kind=kLoop, calls=%fused_computation.70 | loop fusion | flops 16777216 | bytes 100728832 | tf_op jit(solution)/shard_map/mul | solution.py:23
  (215 shorter events, 310.2 us)
Async XLA Ops:
  21.5 14.8 %collective-permute-start = (bf16[64,15,4096]{2,0,1:T(8,128)(2,1)}, bf16[64,15,4096]{2,0,1:T(8,128)(2,1)}, u32[]{:S(2)}, u32[]{:S(2)}) collective-permute-start(bf16[64,15,4096]{2,0,1:T(8,128)(2,1)} %copy.40), channel_id=1, source_target_pairs={{0,1},{1,2},{2,3},{4,5},{5,6},{6,7},{8,9},{9,10},{10,11},{12,13},{... | collective-permute-start | bytes 23592968 | tf_op jit(solution)/shard_map/ppermute | solution.py:11
  62.1 4.3 copy-start.1
  513.6 15.8 %copy-start = (bf16[2,2048,64,16]{1,3,2,0:T(8,128)(2,1)S(1)}, bf16[2,2048,64,16]{1,3,2,0:T(8,128)(2,1)}, u32[]{:S(2)}) copy-start(bf16[2,2048,64,16]{1,3,2,0:T(8,128)(2,1)} %get-tuple-element.135) | copy-start | bytes 25165828
  537.0 263.5 %all-to-all-start = ((bf16[16,1,2,128,64,16]{3,5,4,2,1,0:T(8,128)(2,1)}), bf16[16,1,2,128,64,16]{3,5,4,2,1,0:T(8,128)(2,1)}, u32[]{:S(2)}, u32[]{:S(2)}) async-start(bf16[16,1,2,128,64,16]{3,5,4,2,1,0:T(8,128)(2,1)} %fusion.68), calls=%async_computation | async-start | bytes 16777216 | tf_op jit(solution)/shard_map/all_to_all | solution.py:98
